TPU v7x, 512 devices: a whole 4x4x16 slice. The times are simulated.
512 devices in a mesh: slab: 128 (over y, z, core), sub: 4 (over x).
Axes of the slice: x: 4, y: 4, z: 16, core: 2. Of those that a mesh axis runs over, the one named last changes fastest.
Arguments:
- mode_shapes: bfloat16 [32, 6, 1024, 512], P(None, None, 'slab', 'sub')
- span_stiff: float32 [6, 1024, 512], P(None, 'slab', 'sub'), may hold values from -4 to 4
- chord_stiff: float32 [6, 1024, 512], P(None, 'slab', 'sub'), may hold values from -4 to 4
- span_geo: float32 [1024, 512], P('slab', 'sub'), may hold values from 0.2 to 2
- chord_geo: float32 [1024, 512], P('slab', 'sub'), may hold values from 0.2 to 2
- ground: float32 [6, 1024, 512], P(None, 'slab', 'sub'), may hold values from 0.2 to 2
- chord_len: int32 [1024], replicated, may hold values from 192 to 512, as said below
Outputs:
- adjoint: float32 [32, 6, 1024, 512], P(None, None, 'slab', 'sub')
- residual: float32 [32, 6, 1024, 512], P(None, None, 'slab', 'sub')
Inputs may be any that keep to these rules, and one draw needn't show every extreme that they name: chord_len[0] = 512.
All inputs are finite; a program needn't handle non-finite values.
Results may differ from a plain program's by a relative error of at most 0.0003.
Values sent between devices are 32-bit elements; how exact they have to be, the bound alone decides.
A program may use at most 64 MiB of HBM per device.

v0:
```python
import jax
import jax.numpy as jnp
from jax import lax
from jax.sharding import PartitionSpec as P

ITERS = 2


def from_behind(value, axis, steps):
    count = lax.axis_size(axis)
    initial, last = (max(0, -steps), min(count, count - steps))
    return lax.ppermute(value, axis, [(source, source + steps) for source in range(initial, last)])


def factor_blocks(blocks):
    count = len(blocks)
    factor = [[None] * count for i in range(count)]
    inverse = [None] * count
    for j in range(count):
        running = blocks[j][j]
        for k in range(j):
            running = running - factor[j][k] * factor[j][k]
        diag_root = jnp.sqrt(running)
        factor[j][j] = diag_root
        inverse[j] = 1.0 / diag_root
        for i in range(j + 1, count):
            running = blocks[i][j]
            for k in range(j):
                running = running - factor[i][k] * factor[j][k]
            factor[i][j] = running * inverse[j]
    return (factor, inverse)


def solve_blocks(factor, inverse, vector):
    count = len(inverse)
    forward = []
    for i in range(count):
        running = vector[:, i]
        for j in range(i):
            running = running - factor[i][j][None] * forward[j]
        forward.append(running * inverse[i][None])
    backward = [None] * count
    for i in reversed(range(count)):
        running = forward[i]
        for j in range(i + 1, count):
            running = running - factor[j][i][None] * backward[j]
        backward[i] = running * inverse[i][None]
    return jnp.stack(backward, axis=1)


def neighbours_ahead(field):
    next_station = from_behind(field[:, :, :1, :], "slab", -1)
    next_column = from_behind(field[:, :, :, :1], "sub", -1)
    span_next = jnp.concatenate([field[:, :, 1:, :], next_station], axis=2)
    chord_next = jnp.concatenate([field[:, :, :, 1:], next_column], axis=3)
    return (span_next, chord_next)


def forces_behind(span_forces, chord_forces):
    from_span = from_behind(span_forces[:, :, -1:, :], "slab", 1)
    from_chord = from_behind(chord_forces[:, :, :, -1:], "sub", 1)
    span_part = jnp.concatenate([from_span, span_forces[:, :, :-1, :]], axis=2)
    chord_part = jnp.concatenate([from_chord, chord_forces[:, :, :, :-1]], axis=3)
    return span_part + chord_part


def edge_forces(stiffness, jump, live_mask):
    strain = jnp.sum(stiffness[None] * jump, axis=1) * live_mask[None]
    return stiffness[None] * strain[:, None]


def operate_sent(field, span_stiff, chord_stiff, span_live, chord_live, ground):
    span_next, chord_next = neighbours_ahead(field)
    span_forces = edge_forces(span_stiff, span_next - field, span_live)
    chord_forces = edge_forces(chord_stiff, chord_next - field, chord_live)
    return (
        ground[None] * field - span_forces - chord_forces + forces_behind(span_forces, chord_forces)
    )


def inner_rz(first, second):
    return lax.psum(jnp.sum(first * second, axis=(1, 2, 3)), ("slab", "sub"))


def inner_pq(first, second):
    return lax.psum(jnp.sum(first * second, axis=(1, 2, 3)), ("slab", "sub"))


def body(mode_shapes, span_stiff, chord_stiff, span_geo, chord_geo, ground, chord_len):
    count = ground.shape[0]
    stations = ground.shape[1]
    columns = ground.shape[2]
    row_start = lax.axis_index("slab") * stations
    col_start = lax.axis_index("sub") * columns
    padded_len = jnp.concatenate(
        [jnp.zeros((1,), jnp.int32), chord_len, jnp.zeros((2,), jnp.int32)]
    )
    window = lax.dynamic_slice_in_dim(padded_len, row_start, stations + 2)
    col_global = (col_start + jnp.arange(columns, dtype=jnp.int32))[None, :]
    span_mask_wide = ((col_global < window[:-1, None]) & (col_global < window[1:, None])).astype(
        jnp.float32
    )
    col_wide = (col_start - 1 + jnp.arange(columns + 1, dtype=jnp.int32))[None, :]
    own_len = window[1 : stations + 1, None]
    chord_mask_wide = ((col_wide + 1 < own_len) & (col_wide >= 0)).astype(jnp.float32)
    span_live = span_mask_wide[1:]
    chord_live = chord_mask_wide[:, 1:]
    ghost_span = from_behind(span_stiff[:, stations - 1 :, :], "slab", 1)
    ghost_chord = from_behind(chord_stiff[:, :, columns - 1 :], "sub", 1)
    span_wide = jnp.concatenate([ghost_span, span_stiff], axis=1)
    chord_wide = jnp.concatenate([ghost_chord, chord_stiff], axis=2)
    blocks = []
    for i in range(count):
        block_row = []
        for j in range(count):
            span_pair = span_wide[i] * span_wide[j] * span_mask_wide
            chord_pair = chord_wide[i] * chord_wide[j] * chord_mask_wide
            entry = span_pair[1:] + span_pair[:-1] + chord_pair[:, 1:] + chord_pair[:, :-1]
            if i == j:
                entry = entry + ground[i]
            block_row.append(entry)
        blocks.append(block_row)
    factor, inverse = factor_blocks(blocks)
    mode_field = mode_shapes.astype(jnp.float32)
    span_next, chord_next = neighbours_ahead(mode_field)
    span_jump = span_next - mode_field
    chord_jump = chord_next - mode_field
    span_weight = jnp.sum(span_jump * span_jump, axis=1) * (span_geo * span_live)[None]
    chord_weight = jnp.sum(chord_jump * chord_jump, axis=1) * (chord_geo * chord_live)[None]
    span_load = span_stiff[None] * span_weight[:, None]
    chord_load = chord_stiff[None] * chord_weight[:, None]
    load = forces_behind(span_load, chord_load) - span_load - chord_load
    solution = jnp.zeros_like(load)
    residual = load
    precond = solve_blocks(factor, inverse, residual)
    direction = precond
    precond_norm = inner_rz(residual, precond)
    for step in range(ITERS):
        image = operate_sent(direction, span_stiff, chord_stiff, span_live, chord_live, ground)
        step_size = precond_norm / inner_pq(direction, image)
        solution = solution + step_size[:, None, None, None] * direction
        residual = residual - step_size[:, None, None, None] * image
        if step + 1 < ITERS:
            precond = solve_blocks(factor, inverse, residual)
            norm_next = inner_rz(residual, precond)
            direction = precond + (norm_next / precond_norm)[:, None, None, None] * direction
            precond_norm = norm_next
    return (solution, residual)


def solution(mesh):
    return jax.shard_map(
        body,
        mesh=mesh,
        in_specs=(
            P(None, None, "slab", "sub"),
            P(None, "slab", "sub"),
            P(None, "slab", "sub"),
            P("slab", "sub"),
            P("slab", "sub"),
            P(None, "slab", "sub"),
            P(),
        ),
        out_specs=(P(None, None, "slab", "sub"), P(None, None, "slab", "sub")),
        check_vma=False,
    )
```

profile of v0, /device:TPU:1, one launch (start us, length us, event | category | flops | bytes accessed | tf_op | source)
XLA Modules:
  0.0 413.0 jit_solution(10485907390977975643)
XLA Ops:
  1.4 4.9 %collective-permute-start.4 = (f32[6,1,128]{2,1,0:T(1,128)S(1)}, f32[6,1,128]{2,1,0:T(1,128)S(1)}, u32[]{:S(2)}, u32[]{:S(2)}) collective-permute-start(f32[6,1,128]{2,1,0:T(1,128)S(1)} %slice.527), channel_id=1, source_target_pairs={{0,4},{4,8},{8,12},{12,16},{16,20},{20,24},{24,28},{28,32},{32,36}... | collective-permute-start | bytes 9224 | tf_op jit(solution)/shard_map/ppermute | solution.py:12
  7.1 3.1 collective-permute-start.5
  11.7 1.3 collective-permute-start.2
  13.0 3.3 collective-permute-start
  27.8 2.2 collective-permute-start.1
  30.8 4.0 collective-permute-start.3
  36.2 1.3 fusion.3
  39.2 1.3 collective-permute-start.7
  40.5 3.8 collective-permute-start.6
  46.7 1.6 fusion.9
  49.1 2.1 collective-permute-start.8
  52.5 2.1 copy.16
  54.6 4.4 %collective-permute-start.9 = (f32[32,6,8,1]{0,2,3,1:T(8,128)}, f32[32,6,8,1]{0,2,3,1:T(8,128)}, u32[]{:S(2)}, u32[]{:S(2)}) collective-permute-start(f32[32,6,8,1]{0,2,3,1:T(8,128)} %copy.16), channel_id=1, source_target_pairs={{0,1},{1,2},{2,3},{4,5},{5,6},{6,7},{8,9},{9,10},{10,11},{12,13},{... | collective-permute-start | bytes 18440 | tf_op jit(solution)/shard_map/ppermute | solution.py:12
  59.5 2.0 copy.17
  61.5 2.6 multiply_reduce_fusion.2
  64.1 112.9 %all-reduce = (f32[32]{0:T(128)S(1)}, f32[32]{0:T(128)S(1)}) all-reduce(f32[32]{0:T(128)S(1)} %get-tuple-element.7, f32[32]{0:T(128)S(1)} %get-tuple-element.6), channel_id=1, replica_groups=mesh['slab'=128,'sub'=4] {'slab','sub'}, use_global_device_ids=true, to_apply=%region_3.0 | all-reduce | flops 64 | bytes 512 | tf_op jit(solution)/shard_map/psum | solution.py:82
  177.6 1.3 multiply_subtract_fusion.1
  180.0 98.7 %psum.30 = f32[32]{0:T(128)S(1)} all-reduce(f32[32]{0:T(128)S(1)} %multiply_reduce_fusion.1), channel_id=1, replica_groups=mesh['slab'=128,'sub'=4] {'slab','sub'}, use_global_device_ids=true, to_apply=%region_9.0 | all-reduce | flops 32 | bytes 256 | tf_op jit(solution)/shard_map/psum | solution.py:82
  278.9 2.6 collective-permute-start.10
  281.8 1.3 collective-permute-start.11
  284.3 2.3 collective-permute-done.11
  287.9 1.8 fusion.14
  291.4 4.5 %collective-permute-start.12 = (f32[32,6,1,128]{3,0,2,1:T(8,128)}, f32[32,6,1,128]{3,0,2,1:T(8,128)}, u32[]{:S(2)}, u32[]{:S(2)}) collective-permute-start(f32[32,6,1,128]{3,0,2,1:T(8,128)} %slice.798), channel_id=1, source_target_pairs={{0,4},{4,8},{8,12},{12,16},{16,20},{20,24},{24,28},{28,32},{32,36}... | collective-permute-start | bytes 294920 | tf_op jit(solution)/shard_map/ppermute | solution.py:12
  297.1 1.5 copy.20
  298.6 2.9 collective-permute-start.13
  301.5 2.0 slice.799
  303.5 1.2 copy.21
  304.7 2.7 multiply_reduce_fusion
  307.5 100.6 %psum.31 = f32[32]{0:T(128)S(1)} all-reduce(f32[32]{0:T(128)S(1)} %get-tuple-element.14), channel_id=1, replica_groups=mesh['slab'=128,'sub'=4] {'slab','sub'}, use_global_device_ids=true, to_apply=%region_13.0 | all-reduce | flops 32 | bytes 256 | tf_op jit(solution)/shard_map/psum | solution.py:86
  408.8 1.5 multiply_subtract_fusion
  410.3 1.3 copy.23
  411.7 1.3 copy.22
  (159 shorter events, 31.2 us)
Async XLA Ops:
  1.4 20.2 %collective-permute-start.4 = (f32[6,1,128]{2,1,0:T(1,128)S(1)}, f32[6,1,128]{2,1,0:T(1,128)S(1)}, u32[]{:S(2)}, u32[]{:S(2)}) collective-permute-start(f32[6,1,128]{2,1,0:T(1,128)S(1)} %slice.527), channel_id=1, source_target_pairs={{0,4},{4,8},{8,12},{12,16},{16,20},{20,24},{24,28},{28,32},{32,36}... | collective-permute-start | bytes 9224 | tf_op jit(solution)/shard_map/ppermute | solution.py:12
  7.1 13.7 %collective-permute-start.5 = (f32[6,8,1]{2,1,0:T(8,128)S(1)}, f32[6,8,1]{2,1,0:T(8,128)S(1)}, u32[]{:S(2)}, u32[]{:S(2)}) collective-permute-start(f32[6,8,1]{2,1,0:T(8,128)S(1)} %slice.531), channel_id=1, source_target_pairs={{0,1},{1,2},{2,3},{4,5},{5,6},{6,7},{8,9},{9,10},{10,11},{12,13},{... | collective-permute-start | bytes 584 | tf_op jit(solution)/shard_map/ppermute | solution.py:12
  11.7 14.3 %collective-permute-start.2 = (f32[32,6,8,1]{0,2,3,1:T(8,128)S(1)}, f32[32,6,8,1]{0,2,3,1:T(8,128)S(1)}, u32[]{:S(2)}, u32[]{:S(2)}) collective-permute-start(f32[32,6,8,1]{0,2,3,1:T(8,128)S(1)} %copy.10), channel_id=1, source_target_pairs={{1,0},{2,1},{3,2},{5,4},{6,5},{7,6},{9,8},{10,9},{11,10},{13,12},{... | collective-permute-start | bytes 18440 | tf_op jit(solution)/shard_map/ppermute | solution.py:12
  13.0 13.4 %collective-permute-start = (f32[32,6,1,128]{3,0,2,1:T(8,128)S(1)}, f32[32,6,1,128]{3,0,2,1:T(8,128)S(1)}, u32[]{:S(2)}, u32[]{:S(2)}) collective-permute-start(f32[32,6,1,128]{3,0,2,1:T(8,128)S(1)} %slice.661), channel_id=1, source_target_pairs={{4,0},{8,4},{12,8},{16,12},{20,16},{24,20},{28,24},{32,28},{36,32}... | collective-permute-start | bytes 294920 | tf_op jit(solution)/shard_map/ppermute | solution.py:12
  21.6 3.2 copy-start.7
  26.0 1.0 copy-start.5
  27.8 7.1 %copy-start = (f32[32,6,8,128]{3,0,2,1:T(8,128)}, f32[32,6,8,128]{3,0,2,1:T(8,128)S(1)}, u32[]{:S(2)}) copy-start(f32[32,6,8,128]{3,0,2,1:T(8,128)S(1)} %broadcast_multiply_fusion.5) | copy-start | bytes 2359300
  27.8 2.3 copy-start.21
  27.8 8.3 %collective-permute-start.1 = (f32[32,6,1,128]{3,0,2,1:T(8,128)S(1)}, f32[32,6,1,128]{3,0,2,1:T(8,128)}, u32[]{:S(2)}, u32[]{:S(2)}) collective-permute-start(f32[32,6,1,128]{3,0,2,1:T(8,128)S(1)} %slice.663), channel_id=1, source_target_pairs={{0,4},{4,8},{8,12},{12,16},{16,20},{20,24},{24,28},{28,32},{32,36}... | collective-permute-start | bytes 294920 | tf_op jit(solution)/shard_map/ppermute | solution.py:12
  30.5 4.4 %copy-start.8 = (f32[8,129]{1,0:T(8,128)S(1)}, f32[8,129]{1,0:T(8,128)}, u32[]{:S(2)}) copy-start(f32[8,129]{1,0:T(8,128)} %copy-done.7) | copy-start | bytes 12388
  30.5 4.4 %copy-start.20 = (f32[8,128]{1,0:T(8,128)S(1)}, f32[8,128]{1,0:T(8,128)}, u32[]{:S(2)}) copy-start(f32[8,128]{1,0:T(8,128)} %copy-done.19) | copy-start | bytes 12292
  30.8 4.9 %collective-permute-start.3 = (f32[32,6,8,1]{0,2,3,1:T(8,128)S(1)}, f32[32,6,8,1]{0,2,3,1:T(8,128)S(1)}, u32[]{:S(2)}, u32[]{:S(2)}) collective-permute-start(f32[32,6,8,1]{0,2,3,1:T(8,128)S(1)} %copy.12), channel_id=1, source_target_pairs={{0,1},{1,2},{2,3},{4,5},{5,6},{6,7},{8,9},{9,10},{10,11},{12,13},{... | collective-permute-start | bytes 18440 | tf_op jit(solution)/shard_map/ppermute | solution.py:12
  34.9 1.2 slice-start
  36.1 1.3 copy-start.15
  38.8 5.5 %copy-start.24 = (pred[9,128]{1,0:T(8,128)(4,1)S(1)}, pred[9,128]{1,0:T(8,128)(4,1)}, u32[]{:S(2)}) copy-start(pred[9,128]{1,0:T(8,128)(4,1)} %copy-done.23) | copy-start | bytes 3460
  39.2 6.4 %collective-permute-start.7 = (f32[32,6,8,1]{0,2,3,1:T(8,128)S(1)}, f32[32,6,8,1]{0,2,3,1:T(8,128)S(1)}, u32[]{:S(2)}, u32[]{:S(2)}) collective-permute-start(f32[32,6,8,1]{0,2,3,1:T(8,128)S(1)} %copy.14), channel_id=1, source_target_pairs={{1,0},{2,1},{3,2},{5,4},{6,5},{7,6},{9,8},{10,9},{11,10},{13,12},{... | collective-permute-start | bytes 18440 | tf_op jit(solution)/shard_map/ppermute | solution.py:12
  40.5 6.2 %collective-permute-start.6 = (f32[32,6,1,128]{3,0,2,1:T(8,128)S(1)}, f32[32,6,1,128]{3,0,2,1:T(8,128)S(1)}, u32[]{:S(2)}, u32[]{:S(2)}) collective-permute-start(f32[32,6,1,128]{3,0,2,1:T(8,128)S(1)} %slice.781), channel_id=1, source_target_pairs={{4,0},{8,4},{12,8},{16,12},{20,16},{24,20},{28,24},{32,28},{36,32}... | collective-permute-start | bytes 294920 | tf_op jit(solution)/shard_map/ppermute | solution.py:12
  44.4 3.9 copy-start.17
  48.4 10.6 %copy-start.1 = (f32[32,6,8,128]{3,0,2,1:T(8,128)}, f32[32,6,8,128]{3,0,2,1:T(8,128)S(1)}, u32[]{:S(2)}) copy-start(f32[32,6,8,128]{3,0,2,1:T(8,128)S(1)} %broadcast_multiply_fusion.3) | copy-start | bytes 2359300
  48.4 2.8 copy-start.9
  49.1 12.4 %collective-permute-start.8 = (f32[32,6,1,128]{3,0,2,1:T(8,128)}, f32[32,6,1,128]{3,0,2,1:T(8,128)}, u32[]{:S(2)}, u32[]{:S(2)}) collective-permute-start(f32[32,6,1,128]{3,0,2,1:T(8,128)} %slice.784), channel_id=1, source_target_pairs={{0,4},{4,8},{8,12},{12,16},{16,20},{20,24},{24,28},{28,32},{32,36}... | collective-permute-start | bytes 294920 | tf_op jit(solution)/shard_map/ppermute | solution.py:12
  54.6 4.9 %collective-permute-start.9 = (f32[32,6,8,1]{0,2,3,1:T(8,128)}, f32[32,6,8,1]{0,2,3,1:T(8,128)}, u32[]{:S(2)}, u32[]{:S(2)}) collective-permute-start(f32[32,6,8,1]{0,2,3,1:T(8,128)} %copy.16), channel_id=1, source_target_pairs={{0,1},{1,2},{2,3},{4,5},{5,6},{6,7},{8,9},{9,10},{10,11},{12,13},{... | collective-permute-start | bytes 18440 | tf_op jit(solution)/shard_map/ppermute | solution.py:12
  59.0 2.5 slice-start.1
  177.6 1.4 copy-start.12
  177.6 1.4 copy-start.14
  177.6 1.4 copy-start.16
  278.9 9.0 %collective-permute-start.10 = (f32[32,6,1,128]{3,0,2,1:T(8,128)S(1)}, f32[32,6,1,128]{3,0,2,1:T(8,128)S(1)}, u32[]{:S(2)}, u32[]{:S(2)}) collective-permute-start(f32[32,6,1,128]{3,0,2,1:T(8,128)S(1)} %slice.795), channel_id=1, source_target_pairs={{4,0},{8,4},{12,8},{16,12},{20,16},{24,20},{28,24},{32,28},{36,32}... | collective-permute-start | bytes 294920 | tf_op jit(solution)/shard_map/ppermute | solution.py:12
  281.8 4.8 %collective-permute-start.11 = (f32[32,6,8,1]{0,2,3,1:T(8,128)S(1)}, f32[32,6,8,1]{0,2,3,1:T(8,128)S(1)}, u32[]{:S(2)}, u32[]{:S(2)}) collective-permute-start(f32[32,6,8,1]{0,2,3,1:T(8,128)S(1)} %copy.18), channel_id=1, source_target_pairs={{1,0},{2,1},{3,2},{5,4},{6,5},{7,6},{9,8},{10,9},{11,10},{13,12},{... | collective-permute-start | bytes 18440 | tf_op jit(solution)/shard_map/ppermute | solution.py:12
  287.9 1.8 copy-start.10
  290.5 0.9 copy-start.2
  291.4 13.3 %collective-permute-start.12 = (f32[32,6,1,128]{3,0,2,1:T(8,128)}, f32[32,6,1,128]{3,0,2,1:T(8,128)}, u32[]{:S(2)}, u32[]{:S(2)}) collective-permute-start(f32[32,6,1,128]{3,0,2,1:T(8,128)} %slice.798), channel_id=1, source_target_pairs={{0,4},{4,8},{8,12},{12,16},{16,20},{20,24},{24,28},{28,32},{32,36}... | collective-permute-start | bytes 294920 | tf_op jit(solution)/shard_map/ppermute | solution.py:12
  298.6 4.9 %collective-permute-start.13 = (f32[32,6,8,1]{0,2,3,1:T(8,128)S(1)}, f32[32,6,8,1]{0,2,3,1:T(8,128)S(1)}, u32[]{:S(2)}, u32[]{:S(2)}) collective-permute-start(f32[32,6,8,1]{0,2,3,1:T(8,128)S(1)} %copy.20), channel_id=1, source_target_pairs={{0,1},{1,2},{2,3},{4,5},{5,6},{6,7},{8,9},{9,10},{10,11},{12,13},{... | collective-permute-start | bytes 18440 | tf_op jit(solution)/shard_map/ppermute | solution.py:12
  (14 other events, 9.4 us)
where the time goes:
time: 415 us; the launch traced here: 413 us
  blocking collectives  312 us (75%)
  starting transfers between devices  41.7 us (10%)
  local copies, waits for them, and re-layouts  31.7 us (8%)
  other arithmetic  21.5 us (5%)
  waiting for transfers between devices  4.56 us (1%)
    psum x2, blocking collectives, inner_rz(): return lax.psum(jnp.sum(first * second, axis=(1, 2, 3)), ('slab', 'sub'))  212 us
    psum x1, blocking collectives, inner_pq(): return lax.psum(jnp.sum(first * second, axis=(1, 2, 3)), ('slab', 'sub'))  101 us
    ppermute x14, starting transfers between devices, from_behind(): lax.ppermute(value, axis, [(source, source + steps) for source in range(i...  41.7 us
    unnamed x64, local copies, waits for them, and re-layouts  10.6 us
  transfers between devices with their start and end apart: 14, of which 4 were waited for; matrix products, arithmetic and copies ran while one was open for 6% of the time, Pallas kernels for 0%

commit v1 on v0

--- a/solution.py
+++ b/solution.py
@@ -4,6 +4,12 @@
 from jax.sharding import PartitionSpec as P
 
 ITERS = 2
+
+
+def summed_here(x, axis):
+    blocks = lax.all_gather(x, axis, axis=0, tiled=False)
+    total = blocks.sum(axis=0)
+    return total
 
 
 def from_behind(value, axis, steps):
@@ -79,7 +85,7 @@
 
 
 def inner_rz(first, second):
-    return lax.psum(jnp.sum(first * second, axis=(1, 2, 3)), ("slab", "sub"))
+    return summed_here(jnp.sum(first * second, axis=(1, 2, 3)), ("slab", "sub"))
 
 
 def inner_pq(first, second):

time: 415 us -> 1100 us (2.65)
  waiting for transfers between devices: 4.56 us -> 773 us
  blocking collectives: 312 us -> 215 us
  between operations: 1.34 us -> 14.8 us
    unnamed x0 -> x4, waiting for transfers between devices: none -> 769 us
    psum x2 -> x0, blocking collectives: 212 us -> none  [inner_rz(): return lax.psum(jnp.sum(first * second, axis=(1, 2, 3)), ('slab', 'sub'))]
    psum x1 -> x2, blocking collectives: 101 us -> 215 us  [inner_pq(): return lax.psum(jnp.sum(first * second, axis=(1, 2, 3)), ('slab', 'sub'))]
  transfers between devices with their start and end apart: 14 -> 16, of which waited for: 4 -> 6; matrix products, arithmetic and copies ran while one was open for 6% -> 2% of each run, Pallas kernels for 0% -> 0%
where the time goes in v1:
time: 1100 us
  waiting for transfers between devices  773 us (70%)
  blocking collectives  215 us (20%)
  starting transfers between devices  40.9 us (4%)
  local copies, waits for them, and re-layouts  34.7 us (3%)
  other arithmetic  21.7 us (2%)
  between operations  14.8 us (1%)
    unnamed x4, waiting for transfers between devices  769 us
    psum x2, blocking collectives, inner_pq(): return lax.psum(jnp.sum(first * second, axis=(1, 2, 3)), ('slab', 'sub'))  215 us
    ppermute x14, starting transfers between devices, from_behind(): lax.ppermute(value, axis, [(source, source + steps) for source in range(i...  40.8 us
  transfers between devices with their start and end apart: 16, of which 6 were waited for; matrix products, arithmetic and copies ran while one was open for 2% of the time, Pallas kernels for 0%

profile of v1, /device:TPU:1, one launch (start us, length us, event | category | flops | bytes accessed | tf_op | source)
XLA Modules:
  0.0 1099.9 jit_solution(17322523447961775440)
XLA Ops:
  8.0 4.9 collective-permute-start.4
  13.7 3.1 collective-permute-start.5
  18.3 1.3 collective-permute-start.2
  19.6 3.3 collective-permute-start
  34.4 2.2 collective-permute-start.1
  37.4 4.0 collective-permute-start.3
  42.7 1.3 fusion.3
  45.8 1.3 collective-permute-start.7
  47.1 3.8 collective-permute-start.6
  53.3 1.6 fusion.9
  55.7 2.1 collective-permute-start.8
  59.1 2.1 copy.16
  61.2 4.4 collective-permute-start.9
  66.1 2.0 copy.17
  68.1 2.6 multiply_reduce_fusion.2
  71.7 113.3 %psum.14 = f32[32]{0:T(128)S(1)} all-reduce(f32[32]{0:T(128)S(1)} %get-tuple-element.6), channel_id=1, replica_groups=mesh['slab'=128,'sub'=4] {'slab','sub'}, use_global_device_ids=true, to_apply=%region_7.0 | all-reduce | flops 32 | bytes 256 | tf_op jit(solution)/shard_map/psum | solution.py:92
  185.0 335.1 %all-reduce.5.cloned.1.call-done = f32[16384]{0:T(1024)} async-done(((f32[16384]{0:T(1024)}), f32[16384]{0:T(1024)}) %all-reduce.5.cloned.1.call-update) | async-done | bytes 65552
  521.6 1.3 multiply_subtract_fusion.1
  524.9 433.5 %all-reduce.7.cloned.1.call-done = f32[16384]{0:T(1024)} async-done(((f32[16384]{0:T(1024)}), f32[16384]{0:T(1024)}) %all-reduce.7.cloned.1.call-update) | async-done | bytes 65552
  959.8 2.3 collective-permute-start.10
  962.5 1.3 collective-permute-start.11
  964.9 2.3 collective-permute-done.11
  968.5 1.8 fusion.14
  971.4 4.1 collective-permute-start.12
  976.8 1.5 copy.20
  978.3 2.6 collective-permute-start.13
  980.8 2.0 slice.799
  984.1 2.7 multiply_reduce_fusion
  986.8 101.4 %psum.15 = f32[32]{0:T(128)S(1)} all-reduce(f32[32]{0:T(128)S(1)} %get-tuple-element.12), channel_id=1, replica_groups=mesh['slab'=128,'sub'=4] {'slab','sub'}, use_global_device_ids=true, to_apply=%region_13.0 | all-reduce | flops 32 | bytes 256 | tf_op jit(solution)/shard_map/psum | solution.py:92
  1088.9 1.5 multiply_subtract_fusion
  1090.4 1.3 copy.23
  1091.8 1.3 copy.22
  (176 shorter events, 35.7 us)
Async XLA Ops:
  7.2 512.9 %all-reduce.5.cloned.1.call-start = ((), (), s32[]{:S(2)}) async-start(), calls=%async_computation | async-start | bytes 131072
  8.0 20.2 %collective-permute-start.4 = (f32[6,1,128]{2,1,0:T(1,128)S(1)}, f32[6,1,128]{2,1,0:T(1,128)S(1)}, u32[]{:S(2)}, u32[]{:S(2)}) collective-permute-start(f32[6,1,128]{2,1,0:T(1,128)S(1)} %slice.527), channel_id=1, source_target_pairs={{0,4},{4,8},{8,12},{12,16},{16,20},{20,24},{24,28},{28,32},{32,36}... | collective-permute-start | bytes 9224 | tf_op jit(solution)/shard_map/ppermute | solution.py:18
  13.7 13.8 %collective-permute-start.5 = (f32[6,8,1]{2,1,0:T(8,128)S(1)}, f32[6,8,1]{2,1,0:T(8,128)S(1)}, u32[]{:S(2)}, u32[]{:S(2)}) collective-permute-start(f32[6,8,1]{2,1,0:T(8,128)S(1)} %slice.531), channel_id=1, source_target_pairs={{0,1},{1,2},{2,3},{4,5},{5,6},{6,7},{8,9},{9,10},{10,11},{12,13},{... | collective-permute-start | bytes 584 | tf_op jit(solution)/shard_map/ppermute | solution.py:18
  18.3 14.3 %collective-permute-start.2 = (f32[32,6,8,1]{0,2,3,1:T(8,128)S(1)}, f32[32,6,8,1]{0,2,3,1:T(8,128)S(1)}, u32[]{:S(2)}, u32[]{:S(2)}) collective-permute-start(f32[32,6,8,1]{0,2,3,1:T(8,128)S(1)} %copy.10), channel_id=1, source_target_pairs={{1,0},{2,1},{3,2},{5,4},{6,5},{7,6},{9,8},{10,9},{11,10},{13,12},{... | collective-permute-start | bytes 18440 | tf_op jit(solution)/shard_map/ppermute | solution.py:18
  19.6 13.4 %collective-permute-start = (f32[32,6,1,128]{3,0,2,1:T(8,128)S(1)}, f32[32,6,1,128]{3,0,2,1:T(8,128)S(1)}, u32[]{:S(2)}, u32[]{:S(2)}) collective-permute-start(f32[32,6,1,128]{3,0,2,1:T(8,128)S(1)} %slice.661), channel_id=1, source_target_pairs={{4,0},{8,4},{12,8},{16,12},{20,16},{24,20},{28,24},{32,28},{36,32}... | collective-permute-start | bytes 294920 | tf_op jit(solution)/shard_map/ppermute | solution.py:18
  28.2 3.1 copy-start.9
  34.4 7.1 copy-start.1
  34.4 2.3 copy-start.23
  34.4 8.3 collective-permute-start.1
  37.1 4.4 copy-start.10
  37.1 4.4 copy-start.22
  37.4 4.9 collective-permute-start.3
  42.7 1.3 copy-start.17
  45.4 5.5 copy-start.26
  45.8 6.4 collective-permute-start.7
  47.1 6.2 collective-permute-start.6
  50.9 3.9 copy-start.19
  55.0 10.6 copy-start
  55.0 2.8 copy-start.11
  55.7 12.4 %collective-permute-start.8 = (f32[32,6,1,128]{3,0,2,1:T(8,128)}, f32[32,6,1,128]{3,0,2,1:T(8,128)}, u32[]{:S(2)}, u32[]{:S(2)}) collective-permute-start(f32[32,6,1,128]{3,0,2,1:T(8,128)} %slice.784), channel_id=1, source_target_pairs={{0,4},{4,8},{8,12},{12,16},{16,20},{20,24},{24,28},{28,32},{32,36}... | collective-permute-start | bytes 294920 | tf_op jit(solution)/shard_map/ppermute | solution.py:18
  61.2 4.9 collective-permute-start.9
  65.6 2.5 slice-start
  71.6 886.8 %all-reduce.7.cloned.1.call-start = ((), (), s32[]{:S(2)}) async-start(), calls=%async_computation.1 | async-start | bytes 131072
  521.6 1.4 copy-start.14
  521.6 1.4 copy-start.16
  521.6 1.4 copy-start.18
  959.8 8.7 collective-permute-start.10
  962.5 4.8 collective-permute-start.11
  968.5 1.8 copy-start.12
  968.5 1.8 copy-start.20
  971.4 12.7 %collective-permute-start.12 = (f32[32,6,1,128]{3,0,2,1:T(8,128)}, f32[32,6,1,128]{3,0,2,1:T(8,128)}, u32[]{:S(2)}, u32[]{:S(2)}) collective-permute-start(f32[32,6,1,128]{3,0,2,1:T(8,128)} %slice.798), channel_id=1, source_target_pairs={{0,4},{4,8},{8,12},{12,16},{16,20},{20,24},{24,28},{28,32},{32,36}... | collective-permute-start | bytes 294920 | tf_op jit(solution)/shard_map/ppermute | solution.py:18
  978.3 4.6 collective-permute-start.13
  (18 other events, 13.1 us)
Sparse Core Ops, SparseCore 0:
  71.8 448.2 all-reduce.4
  527.0 431.4 all-reduce.6
